TPU v7x, 256 devices: a whole 4x4x8 slice. The times are simulated.
256 devices in a mesh: cluster: 8 (over z_hi, core), shard: 32 (over x, z_lo, y).
Axes of the slice: x: 4, y: 4, z: 8 (z_hi: 4, z_lo: 2; z = z_hi * 2 + z_lo), core: 2. Of those that a mesh axis runs over, the one named last changes fastest.
Arguments:
- flow_start: float32 [4096, 256], P(('cluster', 'shard')), may hold values from 0 to 1
- demand: float32 [4096, 256], P(('cluster', 'shard')), may hold values from 0.25 to 2
- utility: float32 [4096, 256], P(('cluster', 'shard')), may hold values from 1 to 16
- path_count: int32 [4096], P(('cluster', 'shard')), may hold values from 1 to 256, as said below
- cluster_size: int32 [8], P('cluster'), may hold values from 1 to 16, as said below
- incidence: float32 [8192, 256, 128], P(('cluster', 'shard')), may hold values from 0 to 1, as said below
- inc_path: int32 [8192], P(('cluster', 'shard')), may hold values from 0 to 511, as said below
- inc_edge: int32 [8192], P(('cluster', 'shard')), may hold values from 0 to 6
- capacity: float32 [1792, 128], P(('cluster', 'shard')), may hold values from 0.25 to 4
- dual_start: float32 [1792, 128], P(('cluster', 'shard')), may hold values from 0 to 7
- partner: int32 [8, 3], P('cluster'), may hold values from 0 to 7, as said below
Outputs:
- flows: float32 [4096, 256], P(('cluster', 'shard'))
- duals: float32 [1792, 128], P(('cluster', 'shard'))
Inputs may be any that keep to these rules, and one draw needn't show every extreme that they name: `path_count`: some path block has 256 live paths. `cluster_size`: some cluster has 16. partner[c, k] = q implies partner[q, k] = c; the partners of a cluster are distinct and differ from it. `incidence`: every entry is 0 or 1. Among the 32 incidence blocks of one device, at most 2 have the same value of inc_path // 16, and on every device some value is taken by exactly 2.
All inputs are finite; a program needn't handle non-finite values.
Results may differ from a plain program's by a relative error of at most 0.0001.
Values sent between devices are 32-bit elements; how exact they have to be, the bound alone decides.
A program may use at most 64 MiB of HBM per device.

v0:
```python
import jax
import jax.numpy as jnp
from jax import lax
from jax.sharding import PartitionSpec as P

ITERS = 3


def body(
    flow_start,
    demand,
    utility,
    path_count,
    cluster_size,
    incidence,
    inc_path,
    inc_edge,
    capacity,
    dual_start,
    partner,
):
    exact_mode = lax.Precision.HIGHEST
    block_count, path_width = flow_start.shape
    inc_count = incidence.shape[0]
    edge_width = incidence.shape[2]
    local_blocks = capacity.shape[0]
    slot_count = partner.shape[1]
    interior = local_blocks - slot_count
    clusters = lax.axis_size("cluster")
    norm_bound = max(
        2, inc_count * inc_count * path_width * edge_width // (1024 * local_blocks * block_count)
    )
    capacity_unit = float(max(1, inc_count * path_width // (160 * local_blocks)))
    step_size = 1.0 / (2.0 * norm_bound)
    block_ids = jnp.arange(block_count, dtype=jnp.int32)
    path_ids = jnp.arange(path_width, dtype=jnp.int32)
    live_mask = (
        (block_ids < cluster_size[0])[:, None] & (path_ids[None, :] < path_count[:, None])
    ).astype(jnp.float32)
    edge_pick = (jnp.arange(local_blocks, dtype=jnp.int32)[:, None] == inc_edge[None, :]).astype(
        jnp.float32
    )
    partner_pick = (jnp.arange(clusters, dtype=jnp.int32)[:, None] == partner[0][None, :]).astype(
        jnp.float32
    )

    def twin_of(border):
        outgoing = jnp.dot(partner_pick, border, precision=exact_mode)
        incoming = lax.all_to_all(outgoing, "cluster", split_axis=0, concat_axis=0, tiled=True)
        return jnp.dot(partner_pick.T, incoming, precision=exact_mode)

    cap_border = capacity[interior:]
    dual_border = dual_start[interior:]
    outgoing = jnp.einsum(
        "ck,mke->cme", partner_pick, jnp.stack([cap_border, dual_border]), precision=exact_mode
    )
    incoming = lax.all_to_all(outgoing, "cluster", split_axis=0, concat_axis=0, tiled=True)
    twins = jnp.einsum("ck,cme->mke", partner_pick, incoming, precision=exact_mode)
    limit = capacity_unit * jnp.concatenate(
        [capacity[:interior], 0.5 * (cap_border + twins[0])], axis=0
    )
    duals = jnp.concatenate([dual_start[:interior], 0.5 * (dual_border + twins[1])], axis=0)

    def load_of_rows(picked):
        terms = jnp.einsum("ipe,ip->ie", incidence, picked, precision=exact_mode)
        own_load = jnp.dot(edge_pick, terms, precision=exact_mode)
        border = own_load[interior:]
        return jnp.concatenate([own_load[:interior], border + twin_of(border)], axis=0)

    def total_load(gathered):
        return load_of_rows(jnp.take(gathered, inc_path, axis=0))

    def settle(load, duals_now):
        split = jnp.minimum(limit, load + duals_now)
        return (split, duals_now + load - split)

    flows = jnp.minimum(jnp.maximum(flow_start, 0.0), demand) * live_mask

    def shared_flows(flows_now):
        return lax.all_gather(flows_now, "shard", axis=0, tiled=True)

    load = total_load(shared_flows(flows))
    split, duals = settle(load, duals)
    for iteration in range(ITERS):
        residual = load - split + duals
        residual_picked = jnp.take(residual, inc_edge, axis=0)
        terms = jnp.einsum("ipe,ie->ip", incidence, residual_picked, precision=exact_mode)
        rows_pick = (
            jnp.arange(block_count * lax.axis_size("shard"), dtype=jnp.int32)[:, None]
            == inc_path[None, :]
        ).astype(jnp.float32)
        gradient = lax.psum_scatter(
            jnp.dot(rows_pick, terms, precision=exact_mode),
            "shard",
            scatter_dimension=0,
            tiled=True,
        )
        flows = (
            jnp.minimum(jnp.maximum(flows - step_size * (gradient - utility), 0.0), demand)
            * live_mask
        )
        load = total_load(shared_flows(flows))
        split, duals = settle(load, duals)
    return (flows, duals)


def solution(mesh):
    return jax.shard_map(
        body,
        mesh=mesh,
        in_specs=(
            P(("cluster", "shard"), None),
            P(("cluster", "shard"), None),
            P(("cluster", "shard"), None),
            P(("cluster", "shard")),
            P("cluster"),
            P(("cluster", "shard"), None, None),
            P(("cluster", "shard")),
            P(("cluster", "shard")),
            P(("cluster", "shard"), None),
            P(("cluster", "shard"), None),
            P("cluster", None),
        ),
        out_specs=(P(("cluster", "shard"), None), P(("cluster", "shard"), None)),
        check_vma=False,
    )
```

profile of v0, /device:TPU:1, one launch (start us, length us, event | category | flops | bytes accessed | tf_op | source)
XLA Modules:
  0.0 920.1 jit_solution(6697938760290475055)
XLA Ops:
  9.2 0.8 minimum_select_fusion.3
  10.0 71.7 %all_gather.12 = f32[512,256]{1,0:T(8,128)S(1)} all-gather(f32[16,256]{1,0:T(8,128)S(1)} %minimum_select_fusion.3), channel_id=1, replica_groups=mesh['cluster'=8,'shard'=32] {'shard'}, dimensions={0}, use_global_device_ids=true | all-gather | bytes 540672 | tf_op jit(solution)/shard_map/all_gather | solution.py:80
  82.5 4.4 fusion.18
  87.0 0.9 fusion.39
  87.8 21.9 %all-to-all-start = ((f32[8,1,128]{2,1,0:T(1,128)}), f32[8,1,128]{2,1,0:T(1,128)S(1)}, u32[]{:S(2)}, u32[]{:S(2)}) async-start(f32[8,1,128]{2,1,0:T(1,128)} %bitcast.6), calls=%async_computation | async-start | bytes 8192 | tf_op jit(solution)/shard_map/all_to_all | solution.py:49
  110.7 6.0 all-to-all-done
  116.7 3.9 all-to-all-start.1
  120.8 6.9 all-to-all-done.1
  128.5 5.7 fusion.61
  134.2 1.2 fusion.2
  135.4 128.4 %reduce-scatter.4.cloned.1.call-done = f32[16,256]{1,0:T(8,128)} async-done(((f32[512,256]{1,0:T(8,128)}), f32[16,256]{1,0:T(8,128)}) %reduce-scatter.4.cloned.1.call-update) | async-done | bytes 16400 | tf_op jit(solution)/shard_map/reduce_scatter | solution.py:92
  264.6 65.2 %all_gather.13 = f32[512,256]{1,0:T(8,128)S(1)} all-gather(f32[16,256]{1,0:T(8,128)S(1)} %minimum_select_fusion.2), channel_id=1, replica_groups=mesh['cluster'=8,'shard'=32] {'shard'}, dimensions={0}, use_global_device_ids=true | all-gather | bytes 540672 | tf_op jit(solution)/shard_map/all_gather | solution.py:80
  330.4 4.3 fusion.15
  334.9 0.9 fusion.37
  335.7 46.7 %all-to-all-start.2 = ((f32[8,1,128]{2,1,0:T(1,128)}), f32[8,1,128]{2,1,0:T(1,128)S(1)}, u32[]{:S(2)}, u32[]{:S(2)}) async-start(f32[8,1,128]{2,1,0:T(1,128)} %bitcast.21), calls=%async_computation.3 | async-start | bytes 8192 | tf_op jit(solution)/shard_map/all_to_all | solution.py:49
  382.4 6.9 all-to-all-done.2
  390.2 5.7 fusion.62
  395.9 1.2 fusion.1
  397.1 128.4 %reduce-scatter.6.cloned.1.call-done = f32[16,256]{1,0:T(8,128)} async-done(((f32[512,256]{1,0:T(8,128)}), f32[16,256]{1,0:T(8,128)}) %reduce-scatter.6.cloned.1.call-update) | async-done | bytes 16400 | tf_op jit(solution)/shard_map/reduce_scatter | solution.py:92
  526.2 65.5 %all_gather.14 = f32[512,256]{1,0:T(8,128)S(1)} all-gather(f32[16,256]{1,0:T(8,128)S(1)} %minimum_select_fusion.1), channel_id=1, replica_groups=mesh['cluster'=8,'shard'=32] {'shard'}, dimensions={0}, use_global_device_ids=true | all-gather | bytes 540672 | tf_op jit(solution)/shard_map/all_gather | solution.py:80
  592.4 4.3 fusion.12
  596.8 0.9 fusion.36
  597.7 46.2 %all-to-all-start.3 = ((f32[8,1,128]{2,1,0:T(1,128)}), f32[8,1,128]{2,1,0:T(1,128)S(1)}, u32[]{:S(2)}, u32[]{:S(2)}) async-start(f32[8,1,128]{2,1,0:T(1,128)} %bitcast.30), calls=%async_computation.5 | async-start | bytes 8192 | tf_op jit(solution)/shard_map/all_to_all | solution.py:49
  643.9 6.9 all-to-all-done.3
  651.7 5.7 fusion.63
  657.4 1.2 fusion
  658.6 128.6 %reduce-scatter.8.cloned.1.call-done = f32[16,256]{1,0:T(8,128)} async-done(((f32[512,256]{1,0:T(8,128)}), f32[16,256]{1,0:T(8,128)}) %reduce-scatter.8.cloned.1.call-update) | async-done | bytes 16400 | tf_op jit(solution)/shard_map/reduce_scatter | solution.py:92
  788.0 65.5 %all_gather.15 = f32[512,256]{1,0:T(8,128)S(1)} all-gather(f32[16,256]{1,0:T(8,128)S(1)} %minimum_select_fusion), channel_id=1, replica_groups=mesh['cluster'=8,'shard'=32] {'shard'}, dimensions={0}, use_global_device_ids=true | all-gather | bytes 540672 | tf_op jit(solution)/shard_map/all_gather | solution.py:80
  854.2 4.3 fusion.9
  858.6 0.9 fusion.35
  859.5 46.3 %all-to-all-start.4 = ((f32[8,1,128]{2,1,0:T(1,128)}), f32[8,1,128]{2,1,0:T(1,128)S(1)}, u32[]{:S(2)}, u32[]{:S(2)}) async-start(f32[8,1,128]{2,1,0:T(1,128)} %bitcast.39), calls=%async_computation.7 | async-start | bytes 8192 | tf_op jit(solution)/shard_map/all_to_all | solution.py:49
  905.8 6.9 all-to-all-done.4
  (73 shorter events, 11.5 us)
Async XLA Ops:
  7.2 79.7 %copy-start.6 = (s32[32]{0:T(128)S(1)}, s32[32]{0:T(128)}, u32[]{:S(2)}) copy-start(s32[32]{0:T(128)} %param.22) | copy-start | bytes 388
  7.2 79.8 %copy-start.9 = (s32[1,3]{1,0:T(1,128)S(1)}, s32[1,3]{1,0:T(1,128)}, u32[]{:S(2)}) copy-start(s32[1,3]{1,0:T(1,128)} %param.25) | copy-start | bytes 40
  7.2 102.6 %copy-start.4 = (f32[7,128]{1,0:T(8,128)S(1)}, f32[7,128]{1,0:T(8,128)}, u32[]{:S(2)}) copy-start(f32[7,128]{1,0:T(8,128)} %param.24) | copy-start | bytes 10756
  7.2 102.6 %copy-start.5 = (f32[7,128]{1,0:T(8,128)S(1)}, f32[7,128]{1,0:T(8,128)}, u32[]{:S(2)}) copy-start(f32[7,128]{1,0:T(8,128)} %param.23) | copy-start | bytes 10756
  82.5 51.7 %copy-start.8 = (s32[32]{0:T(128)S(1)}, s32[32]{0:T(128)}, u32[]{:S(2)}) copy-start(s32[32]{0:T(128)} %param.21) | copy-start | bytes 388
  82.5 181.3 %copy-start = (f32[16,256]{1,0:T(8,128)S(1)}, f32[16,256]{1,0:T(8,128)}, u32[]{:S(2)}) copy-start(f32[16,256]{1,0:T(8,128)} %param.16) | copy-start | bytes 49156
  82.5 181.3 %copy-start.1 = (f32[16,256]{1,0:T(8,128)S(1)}, f32[16,256]{1,0:T(8,128)}, u32[]{:S(2)}) copy-start(f32[16,256]{1,0:T(8,128)} %param.17) | copy-start | bytes 49156
  82.5 181.3 %copy-start.2 = (f32[16,256]{1,0:T(8,128)S(1)}, f32[16,256]{1,0:T(8,128)}, u32[]{:S(2)}) copy-start(f32[16,256]{1,0:T(8,128)} %param.15) | copy-start | bytes 49156
  82.5 181.3 %copy-start.7 = (s32[16]{0:T(128)S(1)}, s32[16]{0:T(128)}, u32[]{:S(2)}) copy-start(s32[16]{0:T(128)} %param.18) | copy-start | bytes 196
  87.8 28.8 %all-to-all-start = ((f32[8,1,128]{2,1,0:T(1,128)}), f32[8,1,128]{2,1,0:T(1,128)S(1)}, u32[]{:S(2)}, u32[]{:S(2)}) async-start(f32[8,1,128]{2,1,0:T(1,128)} %bitcast.6), calls=%async_computation | async-start | bytes 8192 | tf_op jit(solution)/shard_map/all_to_all | solution.py:49
  116.7 11.0 %all-to-all-start.1 = ((f32[8,2,128]{2,1,0:T(2,128)}), f32[8,2,128]{2,1,0:T(2,128)S(1)}, u32[]{:S(2)}, u32[]{:S(2)}) async-start(f32[8,2,128]{2,1,0:T(2,128)} %copy.20), calls=%async_computation.1 | async-start | bytes 16384 | tf_op jit(solution)/shard_map/all_to_all | solution.py:57
  120.6 143.2 %reduce-scatter.4.cloned.1.call-start = ((), (), s32[]{:S(2)}) async-start(), calls=%async_computation.8 | async-start | bytes 540672 | tf_op jit(solution)/shard_map/reduce_scatter | solution.py:92
  335.7 53.6 %all-to-all-start.2 = ((f32[8,1,128]{2,1,0:T(1,128)}), f32[8,1,128]{2,1,0:T(1,128)S(1)}, u32[]{:S(2)}, u32[]{:S(2)}) async-start(f32[8,1,128]{2,1,0:T(1,128)} %bitcast.21), calls=%async_computation.3 | async-start | bytes 8192 | tf_op jit(solution)/shard_map/all_to_all | solution.py:49
  382.4 143.0 %reduce-scatter.6.cloned.1.call-start = ((), (), s32[]{:S(2)}) async-start(), calls=%async_computation.9 | async-start | bytes 540672 | tf_op jit(solution)/shard_map/reduce_scatter | solution.py:92
  597.7 53.1 %all-to-all-start.3 = ((f32[8,1,128]{2,1,0:T(1,128)}), f32[8,1,128]{2,1,0:T(1,128)S(1)}, u32[]{:S(2)}, u32[]{:S(2)}) async-start(f32[8,1,128]{2,1,0:T(1,128)} %bitcast.30), calls=%async_computation.5 | async-start | bytes 8192 | tf_op jit(solution)/shard_map/all_to_all | solution.py:49
  643.9 143.2 %reduce-scatter.8.cloned.1.call-start = ((), (), s32[]{:S(2)}) async-start(), calls=%async_computation.10 | async-start | bytes 540672 | tf_op jit(solution)/shard_map/reduce_scatter | solution.py:92
  788.0 125.6 %copy-start.3 = (f32[16,256]{1,0:T(8,128)}, f32[16,256]{1,0:T(8,128)S(1)}, u32[]{:S(2)}) copy-start(f32[16,256]{1,0:T(8,128)S(1)} %minimum_select_fusion) | copy-start | bytes 49156
  859.5 53.3 %all-to-all-start.4 = ((f32[8,1,128]{2,1,0:T(1,128)}), f32[8,1,128]{2,1,0:T(1,128)S(1)}, u32[]{:S(2)}, u32[]{:S(2)}) async-start(f32[8,1,128]{2,1,0:T(1,128)} %bitcast.39), calls=%async_computation.7 | async-start | bytes 8192 | tf_op jit(solution)/shard_map/all_to_all | solution.py:49
Sparse Core Ops, SparseCore 0:
  135.5 128.1 reduce-scatter.3
  397.2 128.2 reduce-scatter.5
  658.7 128.3 reduce-scatter.7
where the time goes:
time: 921 us; the launch traced here: 920 us
  waiting for transfers between devices  419 us (45%)
  blocking collectives  268 us (29%)
  starting transfers between devices  165 us (18%)
  matrix products  43 us (5%)
  between operations  14.6 us (2%)
    reduce_scatter x3, waiting for transfers between devices, body(): lax.psum_scatter(jnp.dot(rows_pick, terms, precision=exact_mode), 'shard'...  385 us
    all_gather x4, blocking collectives, shared_flows(): return lax.all_gather(flows_now, 'shard', axis=0, tiled=True)  268 us
    all_to_all x4, starting transfers between devices, twin_of(): lax.all_to_all(outgoing, 'cluster', split_axis=0, concat_axis=0, tiled=True)  161 us
    all_to_all x4, waiting for transfers between devices, twin_of(): lax.all_to_all(outgoing, 'cluster', split_axis=0, concat_axis=0, tiled=True)  26.7 us
  transfers between devices with their start and end apart: 8, of which 8 were waited for; matrix products, arithmetic and copies ran while one was open for 0% of the time, Pallas kernels for 0%

commit v1 on v0

--- a/solution.py
+++ b/solution.py
@@ -1,9 +1,20 @@
+import functools
 import jax
 import jax.numpy as jnp
 from jax import lax
 from jax.sharding import PartitionSpec as P
 
 ITERS = 3
+
+
+def assign_core(vector, comm_axis):
+    return jnp.concatenate(
+        lax.all_to_all(jnp.stack(lax.axis_size(comm_axis) * [vector], axis=0), comm_axis, 0, 0),
+        axis=0,
+    )
+
+
+name_yards = functools.partial(assign_core, comm_axis="shard")
 
 
 def body(
@@ -77,7 +88,7 @@
     flows = jnp.minimum(jnp.maximum(flow_start, 0.0), demand) * live_mask
 
     def shared_flows(flows_now):
-        return lax.all_gather(flows_now, "shard", axis=0, tiled=True)
+        return name_yards(flows_now)
 
     load = total_load(shared_flows(flows))
     split, duals = settle(load, duals)

time: 921 us -> 664 us (0.72)
  blocking collectives: 268 us -> 35.9 us
  starting transfers between devices: 165 us -> 125 us
  waiting for transfers between devices: 419 us -> 429 us
    all_gather x4 -> x0, blocking collectives: 268 us -> none  [shared_flows(): return lax.all_gather(flows_now, 'shard', axis=0, tiled=True)]
    all_to_all x4, starting transfers between devices: 161 us -> 107 us  [twin_of(): lax.all_to_all(outgoing, 'cluster', split_axis=0, concat_axis=0, tiled=True)]
    all_to_all x0 -> x3, blocking collectives: none -> 35.9 us  [assign_core(): lax.all_to_all(jnp.stack(lax.axis_size(comm_axis) * [vector], axis=0), co...]
  transfers between devices with their start and end apart: 8 -> 9, of which waited for: 8 -> 9; matrix products, arithmetic and copies ran while one was open for 0% -> 1% of each run, Pallas kernels for 0% -> 0%
where the time goes in v1:
time: 664 us; the launch traced here: 663 us
  waiting for transfers between devices  429 us (65%)
  starting transfers between devices  125 us (19%)
  matrix products  44.3 us (7%)
  blocking collectives  35.9 us (5%)
  between operations  14.6 us (2%)
  local copies, waits for them, and re-layouts  7.93 us (1%)
  other arithmetic  7.06 us (1%)
    reduce_scatter x3, waiting for transfers between devices, body(): lax.psum_scatter(jnp.dot(rows_pick, terms, precision=exact_mode), 'shard'...  391 us
    all_to_all x4, starting transfers between devices, twin_of(): lax.all_to_all(outgoing, 'cluster', split_axis=0, concat_axis=0, tiled=True)  107 us
    all_to_all x3, blocking collectives, assign_core(): lax.all_to_all(jnp.stack(lax.axis_size(comm_axis) * [vector], axis=0), co...  35.9 us
    all_to_all x4, waiting for transfers between devices, twin_of(): lax.all_to_all(outgoing, 'cluster', split_axis=0, concat_axis=0, tiled=True)  27.6 us
    dot_general x4, matrix products, load_of_rows(): terms = jnp.einsum('ipe,ip->ie', incidence, picked, precision=exact_mode)  17.3 us
    dot_general x3, matrix products, body(): jnp.einsum('ipe,ie->ip', incidence, residual_picked, precision=exact_mode)  17 us
  transfers between devices with their start and end apart: 9, of which 9 were waited for; matrix products, arithmetic and copies ran while one was open for 1% of the time, Pallas kernels for 0%

profile of v1, /device:TPU:1, one launch (start us, length us, event | category | flops | bytes accessed | tf_op | source)
XLA Modules:
  0.0 663.3 jit_solution(7454245585294808188)
XLA Ops:
  7.9 0.9 fusion.22
  9.5 10.0 %all-to-all-start.2 = ((f32[8,2,128]{2,1,0:T(2,128)}), f32[8,2,128]{2,1,0:T(2,128)S(1)}, u32[]{:S(2)}, u32[]{:S(2)}) async-start(f32[8,2,128]{2,1,0:T(2,128)} %copy.20), calls=%async_computation.2 | async-start | bytes 16384 | tf_op jit(solution)/shard_map/all_to_all | solution.py:68
  21.6 4.9 all-to-all-done.2
  27.3 7.5 %all-to-all-start = ((f32[32,16,256]{2,1,0:T(8,128)}), f32[32,16,256]{2,1,0:T(8,128)S(1)}, u32[]{:S(2)}, u32[]{:S(2)}) async-start(f32[32,16,256]{2,1,0:T(8,128)} %stack.14), calls=%async_computation | async-start | bytes 1048576 | tf_op jit(solution)/shard_map/all_to_all | solution.py:12
  39.0 5.6 all-to-all-done
  45.4 4.4 fusion.18
  50.7 5.9 all-to-all-start.1
  56.6 6.9 %all-to-all-done.1 = f32[8,1,128]{2,1,0:T(1,128)S(1)} async-done(((f32[8,1,128]{2,1,0:T(1,128)}), f32[8,1,128]{2,1,0:T(1,128)S(1)}, u32[]{:S(2)}, u32[]{:S(2)}) %all-to-all-start.1) | async-done | bytes 4128 | tf_op jit(solution)/shard_map/all_to_all | solution.py:60
  64.4 5.7 fusion.61
  70.0 1.2 fusion.2
  71.2 130.2 %reduce-scatter.4.cloned.1.call-done = f32[16,256]{1,0:T(8,128)} async-done(((f32[512,256]{1,0:T(8,128)}), f32[16,256]{1,0:T(8,128)}) %reduce-scatter.4.cloned.1.call-update) | async-done | bytes 16400 | tf_op jit(solution)/shard_map/reduce_scatter | solution.py:103
  202.3 12.0 %all_to_all.73 = f32[32,16,256]{2,1,0:T(8,128)S(1)} all-to-all(f32[32,16,256]{2,1,0:T(8,128)S(1)} %stack.18), channel_id=1, replica_groups=mesh['cluster'=8,'shard'=32] {'shard'}, dimensions={0} | all-to-all | bytes 1048576 | tf_op jit(solution)/shard_map/all_to_all | solution.py:12
  215.0 4.3 fusion.15
  219.4 0.9 fusion.37
  220.3 33.8 %all-to-all-start.4 = ((f32[8,1,128]{2,1,0:T(1,128)}), f32[8,1,128]{2,1,0:T(1,128)S(1)}, u32[]{:S(2)}, u32[]{:S(2)}) async-start(f32[8,1,128]{2,1,0:T(1,128)} %bitcast.23), calls=%async_computation.5 | async-start | bytes 8192 | tf_op jit(solution)/shard_map/all_to_all | solution.py:60
  254.1 6.9 %all-to-all-done.4 = f32[8,1,128]{2,1,0:T(1,128)S(1)} async-done(((f32[8,1,128]{2,1,0:T(1,128)}), f32[8,1,128]{2,1,0:T(1,128)S(1)}, u32[]{:S(2)}, u32[]{:S(2)}) %all-to-all-start.4) | async-done | bytes 4128 | tf_op jit(solution)/shard_map/all_to_all | solution.py:60
  261.9 5.7 fusion.62
  267.5 1.2 fusion.1
  268.8 130.2 %reduce-scatter.6.cloned.1.call-done = f32[16,256]{1,0:T(8,128)} async-done(((f32[512,256]{1,0:T(8,128)}), f32[16,256]{1,0:T(8,128)}) %reduce-scatter.6.cloned.1.call-update) | async-done | bytes 16400 | tf_op jit(solution)/shard_map/reduce_scatter | solution.py:103
  399.8 12.0 %all_to_all.74 = f32[32,16,256]{2,1,0:T(8,128)S(1)} all-to-all(f32[32,16,256]{2,1,0:T(8,128)S(1)} %stack.19), channel_id=1, replica_groups=mesh['cluster'=8,'shard'=32] {'shard'}, dimensions={0} | all-to-all | bytes 1048576 | tf_op jit(solution)/shard_map/all_to_all | solution.py:12
  412.4 4.3 fusion.12
  416.9 0.9 fusion.36
  417.7 33.9 %all-to-all-start.6 = ((f32[8,1,128]{2,1,0:T(1,128)}), f32[8,1,128]{2,1,0:T(1,128)S(1)}, u32[]{:S(2)}, u32[]{:S(2)}) async-start(f32[8,1,128]{2,1,0:T(1,128)} %bitcast.33), calls=%async_computation.8 | async-start | bytes 8192 | tf_op jit(solution)/shard_map/all_to_all | solution.py:60
  451.6 6.9 %all-to-all-done.6 = f32[8,1,128]{2,1,0:T(1,128)S(1)} async-done(((f32[8,1,128]{2,1,0:T(1,128)}), f32[8,1,128]{2,1,0:T(1,128)S(1)}, u32[]{:S(2)}, u32[]{:S(2)}) %all-to-all-start.6) | async-done | bytes 4128 | tf_op jit(solution)/shard_map/all_to_all | solution.py:60
  459.4 5.7 fusion.63
  465.0 1.2 fusion
  466.2 130.2 %reduce-scatter.8.cloned.1.call-done = f32[16,256]{1,0:T(8,128)} async-done(((f32[512,256]{1,0:T(8,128)}), f32[16,256]{1,0:T(8,128)}) %reduce-scatter.8.cloned.1.call-update) | async-done | bytes 16400 | tf_op jit(solution)/shard_map/reduce_scatter | solution.py:103
  597.3 12.0 %all_to_all.75 = f32[32,16,256]{2,1,0:T(8,128)S(1)} all-to-all(f32[32,16,256]{2,1,0:T(8,128)S(1)} %stack.20), channel_id=1, replica_groups=mesh['cluster'=8,'shard'=32] {'shard'}, dimensions={0} | all-to-all | bytes 1048576 | tf_op jit(solution)/shard_map/all_to_all | solution.py:12
  609.9 4.3 fusion.9
  614.4 0.9 fusion.35
  615.2 33.8 %all-to-all-start.8 = ((f32[8,1,128]{2,1,0:T(1,128)}), f32[8,1,128]{2,1,0:T(1,128)S(1)}, u32[]{:S(2)}, u32[]{:S(2)}) async-start(f32[8,1,128]{2,1,0:T(1,128)} %bitcast.43), calls=%async_computation.11 | async-start | bytes 8192 | tf_op jit(solution)/shard_map/all_to_all | solution.py:60
  649.1 6.9 %all-to-all-done.8 = f32[8,1,128]{2,1,0:T(1,128)S(1)} async-done(((f32[8,1,128]{2,1,0:T(1,128)}), f32[8,1,128]{2,1,0:T(1,128)S(1)}, u32[]{:S(2)}, u32[]{:S(2)}) %all-to-all-start.8) | async-done | bytes 4128 | tf_op jit(solution)/shard_map/all_to_all | solution.py:60
  (78 shorter events, 18.0 us)
Async XLA Ops:
  7.2 49.4 %copy-start.4 = (f32[7,128]{1,0:T(8,128)S(1)}, f32[7,128]{1,0:T(8,128)}, u32[]{:S(2)}) copy-start(f32[7,128]{1,0:T(8,128)} %param.24) | copy-start | bytes 10756
  7.2 49.4 %copy-start.5 = (f32[7,128]{1,0:T(8,128)S(1)}, f32[7,128]{1,0:T(8,128)}, u32[]{:S(2)}) copy-start(f32[7,128]{1,0:T(8,128)} %param.23) | copy-start | bytes 10756
  7.2 42.7 %copy-start.9 = (s32[1,3]{1,0:T(1,128)S(1)}, s32[1,3]{1,0:T(1,128)}, u32[]{:S(2)}) copy-start(s32[1,3]{1,0:T(1,128)} %param.25) | copy-start | bytes 40
  7.2 42.5 %copy-start.6 = (s32[32]{0:T(128)S(1)}, s32[32]{0:T(128)}, u32[]{:S(2)}) copy-start(s32[32]{0:T(128)} %param.22) | copy-start | bytes 388
  9.5 17.0 %all-to-all-start.2 = ((f32[8,2,128]{2,1,0:T(2,128)}), f32[8,2,128]{2,1,0:T(2,128)S(1)}, u32[]{:S(2)}, u32[]{:S(2)}) async-start(f32[8,2,128]{2,1,0:T(2,128)} %copy.20), calls=%async_computation.2 | async-start | bytes 16384 | tf_op jit(solution)/shard_map/all_to_all | solution.py:68
  27.3 17.3 %all-to-all-start = ((f32[32,16,256]{2,1,0:T(8,128)}), f32[32,16,256]{2,1,0:T(8,128)S(1)}, u32[]{:S(2)}, u32[]{:S(2)}) async-start(f32[32,16,256]{2,1,0:T(8,128)} %stack.14), calls=%async_computation | async-start | bytes 1048576 | tf_op jit(solution)/shard_map/all_to_all | solution.py:12
  45.3 24.7 %copy-start.8 = (s32[32]{0:T(128)S(1)}, s32[32]{0:T(128)}, u32[]{:S(2)}) copy-start(s32[32]{0:T(128)} %param.21) | copy-start | bytes 388
  45.3 156.1 %copy-start = (f32[16,256]{1,0:T(8,128)S(1)}, f32[16,256]{1,0:T(8,128)}, u32[]{:S(2)}) copy-start(f32[16,256]{1,0:T(8,128)} %param.16) | copy-start | bytes 49156
  45.3 156.1 %copy-start.1 = (f32[16,256]{1,0:T(8,128)S(1)}, f32[16,256]{1,0:T(8,128)}, u32[]{:S(2)}) copy-start(f32[16,256]{1,0:T(8,128)} %param.17) | copy-start | bytes 49156
  45.3 156.1 %copy-start.2 = (f32[16,256]{1,0:T(8,128)S(1)}, f32[16,256]{1,0:T(8,128)}, u32[]{:S(2)}) copy-start(f32[16,256]{1,0:T(8,128)} %param.15) | copy-start | bytes 49156
  45.3 156.1 %copy-start.7 = (s32[16]{0:T(128)S(1)}, s32[16]{0:T(128)}, u32[]{:S(2)}) copy-start(s32[16]{0:T(128)} %param.18) | copy-start | bytes 196
  50.7 12.8 %all-to-all-start.1 = ((f32[8,1,128]{2,1,0:T(1,128)}), f32[8,1,128]{2,1,0:T(1,128)S(1)}, u32[]{:S(2)}, u32[]{:S(2)}) async-start(f32[8,1,128]{2,1,0:T(1,128)} %bitcast.7), calls=%async_computation.1 | async-start | bytes 8192 | tf_op jit(solution)/shard_map/all_to_all | solution.py:60
  56.6 144.9 %reduce-scatter.4.cloned.1.call-start = ((), (), s32[]{:S(2)}) async-start(), calls=%async_computation.12 | async-start | bytes 540672 | tf_op jit(solution)/shard_map/reduce_scatter | solution.py:103
  220.3 40.7 %all-to-all-start.4 = ((f32[8,1,128]{2,1,0:T(1,128)}), f32[8,1,128]{2,1,0:T(1,128)S(1)}, u32[]{:S(2)}, u32[]{:S(2)}) async-start(f32[8,1,128]{2,1,0:T(1,128)} %bitcast.23), calls=%async_computation.5 | async-start | bytes 8192 | tf_op jit(solution)/shard_map/all_to_all | solution.py:60
  254.1 144.8 %reduce-scatter.6.cloned.1.call-start = ((), (), s32[]{:S(2)}) async-start(), calls=%async_computation.13 | async-start | bytes 540672 | tf_op jit(solution)/shard_map/reduce_scatter | solution.py:103
  417.7 40.8 %all-to-all-start.6 = ((f32[8,1,128]{2,1,0:T(1,128)}), f32[8,1,128]{2,1,0:T(1,128)S(1)}, u32[]{:S(2)}, u32[]{:S(2)}) async-start(f32[8,1,128]{2,1,0:T(1,128)} %bitcast.33), calls=%async_computation.8 | async-start | bytes 8192 | tf_op jit(solution)/shard_map/all_to_all | solution.py:60
  451.6 144.8 %reduce-scatter.8.cloned.1.call-start = ((), (), s32[]{:S(2)}) async-start(), calls=%async_computation.14 | async-start | bytes 540672 | tf_op jit(solution)/shard_map/reduce_scatter | solution.py:103
  597.2 59.6 %copy-start.3 = (f32[16,256]{1,0:T(8,128)}, f32[16,256]{1,0:T(8,128)S(1)}, u32[]{:S(2)}) copy-start(f32[16,256]{1,0:T(8,128)S(1)} %minimum_select_fusion) | copy-start | bytes 49156
  615.2 40.7 %all-to-all-start.8 = ((f32[8,1,128]{2,1,0:T(1,128)}), f32[8,1,128]{2,1,0:T(1,128)S(1)}, u32[]{:S(2)}, u32[]{:S(2)}) async-start(f32[8,1,128]{2,1,0:T(1,128)} %bitcast.43), calls=%async_computation.11 | async-start | bytes 8192 | tf_op jit(solution)/shard_map/all_to_all | solution.py:60
Sparse Core Ops, SparseCore 0:
  71.4 130.0 reduce-scatter.3
  268.9 129.9 reduce-scatter.5
  466.4 130.0 reduce-scatter.7
